TPU v7x, 32 devices: a whole 2x2x4 slice. The times are simulated.
32 devices in a mesh: term: 2 (over x), sector: 16 (over z, y, core).
Axes of the slice: x: 2, y: 2, z: 4, core: 2. Of those that a mesh axis runs over, the one named last changes fastest.
Arguments:
- psi_start: bfloat16 [128, 256, 256], P('sector'), may hold values from -6 to 6
- left_env: bfloat16 [6, 128, 256, 256], P('term', 'sector')
- right_env: bfloat16 [6, 128, 256, 256], P('term', 'sector')
- connect: int32 [6, 128], P('term', 'sector'), may hold values from 0 to 127, as said below
- sector_dims: int32 [2, 128], P(None, 'sector'), may hold values from 64 to 256
- precond: bfloat16 [128, 256, 256], P('sector'), may hold values from 0.5 to 4
Outputs:
- projected: float32 [3, 3], replicated
- last_vector: float32 [128, 256, 256], P('sector', 'term')
- new_env: bfloat16 [6, 128, 256, 256], P('term', 'sector')
Inputs may be any that keep to these rules, and one draw needn't show every extreme that they name: connect[t, s] differs from s by at most 8.
All inputs are finite; a program needn't handle non-finite values.
Results may differ from a plain program's by a relative error of at most 0.012.
Values may be sent and summed in bfloat16 or wider, within the bound.
A program may use at most 128 MiB of HBM per device.

v0:
```python
import jax
import jax.numpy as jnp
from jax import lax
from jax.sharding import PartitionSpec as P

epsilon = 1e-06


def with_halo(block, sides, width):
    for axis, dim in sides:
        count = lax.axis_size(axis)
        forward = [(i, i + 1) for i in range(count - 1)]
        backward = [(target, source) for source, target in forward]
        low = lax.ppermute(
            lax.slice_in_dim(block, block.shape[dim] - width, None, axis=dim), axis, forward
        )
        high = lax.ppermute(lax.slice_in_dim(block, 0, width, axis=dim), axis, backward)
        block = jnp.concatenate([low, block, high], axis=dim)
    return block


def on_device(psi_start, left_env, right_env, connect, sector_dims, precond):
    blocks = psi_start.shape[0]
    width = psi_start.shape[1]
    devices = lax.axis_size("sector")
    pieces = lax.axis_size("term")
    terms_here = left_env.shape[0]
    entries = float(blocks * devices * width * width)
    local_source = connect - (lax.axis_index("sector") * blocks - blocks)
    share = width // pieces
    share_start = lax.axis_index("term") * share
    row_ids = lax.broadcasted_iota(jnp.int32, (blocks, width, width), 1)
    col_ids = lax.broadcasted_iota(jnp.int32, (blocks, width, width), 2)
    keep = (row_ids < sector_dims[0][:, None, None]) & (col_ids < sector_dims[1][:, None, None])
    mask = keep.astype(jnp.float32)
    start_rows = psi_start.astype(jnp.float32) * mask
    divisor = precond.astype(jnp.float32)

    def totals(values):
        stacked = jnp.stack(values)
        summed = lax.psum(stacked, "sector")
        return summed / entries

    norm_start = totals([jnp.sum(start_rows * start_rows)])[0]
    basis = [start_rows / jnp.sqrt(norm_start + epsilon)]
    sigmas = []
    env_list = []
    for which in range(3):
        vector_b = basis[which].astype(jnp.bfloat16)
        extended = with_halo(vector_b, (("sector", 0),), blocks)
        with_env = which == 2
        total = jnp.zeros((blocks, width, width), jnp.float32)
        own_blocks = extended[blocks : 2 * blocks]
        envs = []
        for apply_which in range(terms_here):
            source = jnp.take(extended, local_source[apply_which], axis=0)
            half = jnp.einsum(
                "sij,sjk->sik", left_env[apply_which], source, preferred_element_type=jnp.float32
            ).astype(jnp.bfloat16)
            total = total + jnp.einsum(
                "sik,slk->sil", half, right_env[apply_which], preferred_element_type=jnp.float32
            )
            if with_env:
                env_one = jnp.einsum(
                    "sji,sjk->sik", own_blocks, half, preferred_element_type=jnp.float32
                ) * width ** (-0.5)
                envs.append(env_one.astype(jnp.bfloat16))
        sigma = lax.psum(total, "term")
        sigma, env_list = (sigma * mask, envs)
        sigmas.append(sigma)
        if which < 2:
            theta = totals([jnp.sum(basis[which] * sigma)])[0]
            corr = (sigma - theta * basis[which]) / divisor
            correlations = totals([jnp.sum(member * corr) for member in basis])
            for position in range(len(basis)):
                corr = corr - correlations[position] * basis[position]
            length = totals([jnp.sum(corr * corr)])[0]
            basis.append(corr / jnp.sqrt(length + epsilon))
    products = totals([jnp.sum(basis[row] * sigmas[col]) for row in range(3) for col in range(3)])
    projected = products.reshape(3, 3)
    last_vector = lax.dynamic_slice_in_dim(basis[2], share_start, share, 1)
    return (projected, last_vector, jnp.stack(env_list))


def solution(mesh):
    placed = (
        P("sector", None, None),
        P("term", "sector", None, None),
        P("term", "sector", None, None),
        P("term", "sector"),
        P(None, "sector"),
        P("sector", None, None),
    )
    return jax.shard_map(
        on_device,
        mesh=mesh,
        in_specs=placed,
        out_specs=(P(), P("sector", "term", None), P("term", "sector", None, None)),
        check_vma=False,
    )
```

profile of v0, /device:TPU:0, one launch (start us, length us, event | category | flops | bytes accessed | tf_op | source)
XLA Modules:
  0.0 646.5 jit_solution(17308843335064194327)
XLA Ops:
  8.0 2.4 multiply_reduce_fusion.14
  10.4 35.6 %psum.77 = f32[1]{0:T(128)} all-reduce(f32[1]{0:T(128)} %bitcast.2), channel_id=1, replica_groups=mesh['term'=2,'sector'=16] {'sector'}, use_global_device_ids=true, to_apply=%region_1.0 | all-reduce | flops 1 | bytes 8 | tf_op jit(solution)/shard_map/psum | solution.py:41
  46.7 1.8 fusion.119
  54.5 2.0 pad_maximum_fusion
  59.7 1.6 gather_fusion.2
  61.3 4.2 fusion.3
  65.5 3.7 fusion.2
  69.2 5.0 add_add_fusion.2
  74.3 79.1 %all-reduce.4.cloned.1.call-done = f32[8,256,256]{2,1,0:T(8,128)} async-done(((f32[8,256,256]{2,1,0:T(8,128)}), f32[8,256,256]{2,1,0:T(8,128)}) %all-reduce.4.cloned.1.call-update) | async-done | bytes 2097168 | tf_op jit(solution)/shard_map/psum | solution.py:68
  153.4 3.0 multiply_reduce_fusion.13
  156.5 33.6 %psum.79 = f32[1]{0:T(128)} all-reduce(f32[1]{0:T(128)} %bitcast.13), channel_id=1, replica_groups=mesh['term'=2,'sector'=16] {'sector'}, use_global_device_ids=true, to_apply=%region_4.6 | all-reduce | flops 1 | bytes 8 | tf_op jit(solution)/shard_map/psum | solution.py:41
  190.8 2.8 multiply_reduce_fusion.12
  193.6 30.1 %psum.80 = f32[1]{0:T(128)} all-reduce(f32[1]{0:T(128)} %bitcast.15), channel_id=1, replica_groups=mesh['term'=2,'sector'=16] {'sector'}, use_global_device_ids=true, to_apply=%region_6.8 | all-reduce | flops 1 | bytes 8 | tf_op jit(solution)/shard_map/psum | solution.py:41
  224.3 3.6 multiply_reduce_fusion.11
  227.9 30.1 %psum.81 = f32[1]{0:T(128)} all-reduce(f32[1]{0:T(128)} %bitcast.17), channel_id=1, replica_groups=mesh['term'=2,'sector'=16] {'sector'}, use_global_device_ids=true, to_apply=%region_8.10 | all-reduce | flops 1 | bytes 8 | tf_op jit(solution)/shard_map/psum | solution.py:41
  258.9 1.8 collective-permute-start.2
  263.0 2.4 collective-permute-done.3
  265.3 1.8 pad_maximum_fusion.1
  267.2 3.5 gather_fusion.4
  270.6 3.5 gather_fusion.3
  274.1 3.5 gather_fusion.5
  277.6 4.0 fusion.5
  281.6 4.0 fusion.4
  285.6 5.3 add_add_fusion.1
  291.2 79.4 %all-reduce.6.cloned.1.call-done = f32[8,256,256]{2,1,0:T(8,128)} async-done(((f32[8,256,256]{2,1,0:T(8,128)}), f32[8,256,256]{2,1,0:T(8,128)}) %all-reduce.6.cloned.1.call-update) | async-done | bytes 2097168 | tf_op jit(solution)/shard_map/psum | solution.py:68
  370.5 2.9 multiply_reduce_fusion.9
  373.4 33.6 %psum.83 = f32[1]{0:T(128)} all-reduce(f32[1]{0:T(128)} %bitcast.20), channel_id=1, replica_groups=mesh['term'=2,'sector'=16] {'sector'}, use_global_device_ids=true, to_apply=%region_12.14 | all-reduce | flops 1 | bytes 8 | tf_op jit(solution)/shard_map/psum | solution.py:41
  407.7 3.9 multiply_reduce_fusion.8
  413.0 29.5 %psum.84 = f32[2]{0:T(128)S(1)} all-reduce(f32[2]{0:T(128)S(1)} %pad_maximum_fusion.4), channel_id=1, replica_groups=mesh['term'=2,'sector'=16] {'sector'}, use_global_device_ids=true, to_apply=%region_15.17 | all-reduce | flops 2 | bytes 16 | tf_op jit(solution)/shard_map/psum | solution.py:41
  443.1 6.4 multiply_reduce_fusion.6
  449.5 30.1 %psum.85 = f32[1]{0:T(128)} all-reduce(f32[1]{0:T(128)} %bitcast.26), channel_id=1, replica_groups=mesh['term'=2,'sector'=16] {'sector'}, use_global_device_ids=true, to_apply=%region_17.19 | all-reduce | flops 1 | bytes 8 | tf_op jit(solution)/shard_map/psum | solution.py:41
  480.3 3.2 fusion.121
  483.5 1.8 collective-permute-start.4
  487.5 2.4 collective-permute-done.5
  489.9 1.8 pad_maximum_fusion.2
  491.7 3.5 gather_fusion.6
  495.2 3.5 gather_fusion.7
  498.7 3.5 gather_fusion.8
  502.2 2.3 convolution_convert_fusion.8
  504.7 2.2 convolution_convert_fusion.7
  507.5 1.7 copy-done.5
  510.2 1.9 add_add_fusion
  512.2 2.4 constant_dynamic-slice_fusion
  519.2 72.6 %all-reduce.8.cloned.1.call-done = f32[8,256,256]{2,1,0:T(8,128)} async-done(((f32[8,256,256]{2,1,0:T(8,128)}), f32[8,256,256]{2,1,0:T(8,128)}) %all-reduce.8.cloned.1.call-update) | async-done | bytes 2097168 | tf_op jit(solution)/shard_map/psum | solution.py:68
  591.7 4.9 multiply_reduce_fusion
  596.6 5.8 stack.81
  602.4 3.9 pad_maximum_fusion.3
  606.3 33.0 %psum.87 = f32[9]{0:T(128)S(1)} all-reduce(f32[9]{0:T(128)S(1)} %stack.81), channel_id=1, replica_groups=mesh['term'=2,'sector'=16] {'sector'}, use_global_device_ids=true, to_apply=%region_25.27 | all-reduce | flops 9 | bytes 72 | tf_op jit(solution)/shard_map/psum | solution.py:41
  (66 shorter events, 23.9 us)
Async XLA Ops:
  7.2 44.0 %copy-start.16 = (s32[3,8]{1,0:T(4,128)S(1)}, s32[3,8]{1,0:T(4,128)}, u32[]{:S(2)}) copy-start(s32[3,8]{1,0:T(4,128)} %param.11) | copy-start | bytes 292
  7.2 146.2 %all-reduce.4.cloned.1.call-start = ((), (), s32[]{:S(2)}) async-start(), calls=%async_computation | async-start | bytes 4194304 | tf_op jit(solution)/shard_map/psum | solution.py:68
  48.5 3.6 copy-start.10
  48.5 3.6 collective-permute-start
  49.9 4.7 collective-permute-start.1
  52.1 1.0 copy-start.15
  61.3 4.2 copy-start.4
  74.2 79.2 %copy-start = (bf16[8,256,256]{2,1,0:T(8,128)(2,1)S(1)}, bf16[8,256,256]{2,1,0:T(8,128)(2,1)}, u32[]{:S(2)}) copy-start(bf16[8,256,256]{2,1,0:T(8,128)(2,1)} %param.8) | copy-start | bytes 3145732
  74.2 296.3 %all-reduce.6.cloned.1.call-start = ((), (), s32[]{:S(2)}) async-start(), calls=%async_computation.1 | async-start | bytes 4194304 | tf_op jit(solution)/shard_map/psum | solution.py:68
  153.4 37.3 %copy-start.1 = (f32[8,256,256]{2,1,0:T(8,128)S(1)}, f32[8,256,256]{2,1,0:T(8,128)}, u32[]{:S(2)}) copy-start(f32[8,256,256]{2,1,0:T(8,128)} %all-reduce.4.cloned.1.call-done) | copy-start | bytes 6291460
  258.9 4.0 collective-permute-start.2
  260.8 4.6 collective-permute-start.3
  290.9 300.8 %all-reduce.8.cloned.1.call-start = ((), (), s32[]{:S(2)}) async-start(), calls=%async_computation.2 | async-start | bytes 4194304 | tf_op jit(solution)/shard_map/psum | solution.py:68
  483.5 6.4 copy-start.2
  483.5 4.0 collective-permute-start.4
  485.3 4.6 collective-permute-start.5
  502.2 2.5 copy-start.13
  504.7 5.0 copy-start.6
  504.7 2.2 copy-start.14
  506.9 2.8 copy-start.8
  506.9 2.3 copy-start.5
  509.2 1.0 copy-start.11
  512.1 2.4 copy-start.3
  512.2 2.4 copy-start.7
  514.6 1.6 copy-start.9
  516.2 1.5 copy-start.12
Sparse Core Ops, SparseCore 0:
  74.4 79.0 all-reduce.3
  291.0 79.4 all-reduce.5
  512.3 79.4 all-reduce.7
where the time goes:
time: 648 us; the launch traced here: 646 us
  blocking collectives  256 us (40%)
  waiting for transfers between devices  240 us (37%)
  other arithmetic  46.1 us (7%)
  local copies, waits for them, and re-layouts  38.9 us (6%)
  matrix products  38.6 us (6%)
  between operations  18 us (3%)
  starting transfers between devices  9.19 us (1%)
    psum x8, blocking collectives, totals(): summed = lax.psum(stacked, 'sector')  256 us
    psum x3, waiting for transfers between devices, on_device(): sigma = lax.psum(total, 'term')  231 us
    dot_general x9, matrix products, on_device(): jnp.einsum('sik,slk->sil', half, right_env[apply_which], preferred_elemen...  29 us
    gather x9, local copies, waits for them, and re-layouts, on_device(): source = jnp.take(extended, local_source[apply_which], axis=0)  25.7 us
  transfers between devices with their start and end apart: 9, of which 9 were waited for; matrix products, arithmetic and copies ran while one was open for 1% of the time, Pallas kernels for 0%

commit v1 on v0

--- a/solution.py
+++ b/solution.py
@@ -38,7 +38,11 @@
 
     def totals(values):
         stacked = jnp.stack(values)
-        summed = lax.psum(stacked, "sector")
+        summed = stacked
+        for hop in (1, 2, 4, 8):
+            summed = summed + lax.ppermute(
+                summed, "sector", [(dev, dev ^ hop) for dev in range(16)]
+            )
         return summed / entries
 
     norm_start = totals([jnp.sum(start_rows * start_rows)])[0]

time: 648 us -> 517 us (0.80)
  blocking collectives: 256 us -> 0 us
  starting transfers between devices: 9.19 us -> 79 us
  waiting for transfers between devices: 240 us -> 290 us
  between operations: 18 us -> 32.7 us
  other arithmetic: 46.1 us -> 38.2 us
    psum x8 -> x0, blocking collectives: 256 us -> none  [totals(): summed = lax.psum(stacked, 'sector')]
    ppermute x0 -> x32, starting transfers between devices: none -> 70.5 us  [totals(): lax.ppermute(summed, 'sector', [(dev, dev ^ hop) for dev in range(16)])]
    ppermute x0 -> x32, waiting for transfers between devices: none -> 34.8 us  [totals(): lax.ppermute(summed, 'sector', [(dev, dev ^ hop) for dev in range(16)])]
    psum x3, waiting for transfers between devices: 231 us -> 241 us  [on_device(): sigma = lax.psum(total, 'term')]
  transfers between devices with their start and end apart: 9 -> 41, of which waited for: 9 -> 41; matrix products, arithmetic and copies ran while one was open for 1% -> 1% of each run, Pallas kernels for 0% -> 0%
where the time goes in v1:
time: 517 us; the launch traced here: 515 us
  waiting for transfers between devices  290 us (56%)
  starting transfers between devices  79 us (15%)
  local copies, waits for them, and re-layouts  40.3 us (8%)
  other arithmetic  38.2 us (7%)
  matrix products  35.7 us (7%)
  between operations  32.7 us (6%)
    psum x3, waiting for transfers between devices, on_device(): sigma = lax.psum(total, 'term')  241 us
    ppermute x32, starting transfers between devices, totals(): lax.ppermute(summed, 'sector', [(dev, dev ^ hop) for dev in range(16)])  70.5 us
    ppermute x32, waiting for transfers between devices, totals(): lax.ppermute(summed, 'sector', [(dev, dev ^ hop) for dev in range(16)])  34.8 us
    dot_general x9, matrix products, on_device(): jnp.einsum('sik,slk->sil', half, right_env[apply_which], preferred_elemen...  29.1 us
    gather x9, local copies, waits for them, and re-layouts, on_device(): source = jnp.take(extended, local_source[apply_which], axis=0)  25.7 us
    ppermute x3, waiting for transfers between devices, with_halo(): lax.ppermute(lax.slice_in_dim(block, 0, width, axis=dim), axis, backward)  11.5 us
  transfers between devices with their start and end apart: 41, of which 41 were waited for; matrix products, arithmetic and copies ran while one was open for 1% of the time, Pallas kernels for 0%

profile of v1, /device:TPU:0, one launch (start us, length us, event | category | flops | bytes accessed | tf_op | source)
XLA Modules:
  0.0 515.5 jit_solution(2954694113370711308)
XLA Ops:
  8.0 2.4 multiply_reduce_fusion.14
  13.1 4.2 collective-permute-start.1
  18.2 3.4 collective-permute-start.2
  22.4 4.4 collective-permute-start.3
  34.1 3.5 collective-permute-done.5
  44.4 4.1 fusion.3
  48.5 3.7 fusion.2
  52.2 5.0 add_add_fusion.2
  57.3 83.9 %all-reduce.4.cloned.1.call-done = f32[8,256,256]{2,1,0:T(8,128)} async-done(((f32[8,256,256]{2,1,0:T(8,128)}), f32[8,256,256]{2,1,0:T(8,128)}) %all-reduce.4.cloned.1.call-update) | async-done | bytes 2097168 | tf_op jit(solution)/shard_map/psum | solution.py:72
  141.2 3.1 multiply_reduce_fusion.13
  146.7 2.8 collective-permute-start.7
  150.9 2.8 collective-permute-start.8
  155.2 3.8 collective-permute-start.9
  164.5 2.8 collective-permute-start.11
  168.7 2.8 collective-permute-start.12
  172.9 3.8 collective-permute-start.13
  182.5 2.8 collective-permute-start.15
  186.7 2.8 collective-permute-start.16
  191.0 3.8 collective-permute-start.17
  199.9 4.0 collective-permute-done.19
  205.7 3.5 gather_fusion.4
  209.2 3.5 gather_fusion.3
  212.7 3.5 gather_fusion.5
  216.1 4.0 fusion.5
  220.1 4.0 fusion.4
  224.1 5.3 %add_add_fusion.1 = f32[8,256,256]{2,1,0:T(8,128)} fusion(f32[8,256,256]{2,1,0:T(8,128)} %fusion.4, f32[8,256,256]{2,1,0:T(8,128)} %fusion.5, bf16[8,256,256]{2,1,0:T(8,128)(2,1)} %gather_fusion.5, pred[8]{0:T(512)(128)(4,1)S(1)} %get-tuple-element.19, bf16[3,8,256,256]{3,2,1,0:T(8,128)(2,1)} %param.10, bf16[3,8,256,256]{3,2,1,0:T(8,128)(2,1)} %param.9), kind=kOutput, calls=%fused_computation.31 | convolution fusion | flops 538968064 | bytes 9437192 | tf_op jit(solution)/shard_map/sik,slk->sil/dot_general | solution.py:64
  229.5 82.3 %all-reduce.6.cloned.1.call-done = f32[8,256,256]{2,1,0:T(8,128)} async-done(((f32[8,256,256]{2,1,0:T(8,128)}), f32[8,256,256]{2,1,0:T(8,128)}) %all-reduce.6.cloned.1.call-update) | async-done | bytes 2097168 | tf_op jit(solution)/shard_map/psum | solution.py:72
  311.8 3.0 multiply_reduce_fusion.9
  317.4 2.8 collective-permute-start.21
  321.7 2.8 collective-permute-start.22
  326.0 3.8 collective-permute-start.23
  331.3 2.6 multiply_reduce_fusion.8
  346.0 2.4 collective-permute-start.27
  351.1 3.4 multiply_reduce_fusion.6
  357.1 2.8 collective-permute-start.29
  361.4 2.8 collective-permute-start.30
  365.7 3.8 collective-permute-start.31
  376.2 4.0 collective-permute-done.33
  382.0 3.5 gather_fusion.6
  385.5 3.5 gather_fusion.7
  389.0 3.6 gather_fusion.8
  392.5 2.3 convolution_convert_fusion.8
  395.0 2.2 convolution_convert_fusion.7
  402.6 2.4 constant_dynamic-slice_fusion
  410.0 74.9 %all-reduce.8.cloned.1.call-done = f32[8,256,256]{2,1,0:T(8,128)} async-done(((f32[8,256,256]{2,1,0:T(8,128)}), f32[8,256,256]{2,1,0:T(8,128)}) %all-reduce.8.cloned.1.call-update) | async-done | bytes 2097168 | tf_op jit(solution)/shard_map/psum | solution.py:72
  484.9 4.9 multiply_reduce_fusion
  489.8 5.7 %stack.81 = f32[9]{0:T(128)S(1)} concatenate(f32[1]{0:T(128)} %bitcast.13, f32[1]{0:T(128)} %bitcast.19, f32[1]{0:T(128)} %bitcast.28, f32[1]{0:T(128)} %bitcast.29, f32[1]{0:T(128)} %bitcast.20, f32[1]{0:T(128)} %bitcast.30, f32[1]{0:T(128)} %bitcast.31, f32[1]{0:T(128)} %bitcast.32, f32[1]{0:T(128)} %bitcast.33), dimensions={0} | concatenate | bytes 72 | tf_op jit(solution)/shard_map/stack | solution.py:40
  503.8 2.4 collective-permute-start.37
  (136 shorter events, 87.0 us)
Async XLA Ops:
  7.2 25.0 %copy-start.20 = (s32[3,8]{1,0:T(4,128)S(1)}, s32[3,8]{1,0:T(4,128)}, u32[]{:S(2)}) copy-start(s32[3,8]{1,0:T(4,128)} %param.11) | copy-start | bytes 292
  7.2 134.0 %all-reduce.4.cloned.1.call-start = ((), (), s32[]{:S(2)}) async-start(), calls=%async_computation | async-start | bytes 4194304 | tf_op jit(solution)/shard_map/psum | solution.py:72
  10.4 1.4 collective-permute-start
  13.1 4.4 collective-permute-start.1
  18.2 3.6 collective-permute-start.2
  22.4 4.6 collective-permute-start.3
  29.5 3.6 collective-permute-start.4
  30.9 6.7 %collective-permute-start.5 = (bf16[8,256,256]{2,1,0:T(8,128)(2,1)S(1)}, bf16[8,256,256]{2,1,0:T(8,128)(2,1)}, u32[]{:S(2)}, u32[]{:S(2)}) collective-permute-start(bf16[8,256,256]{2,1,0:T(8,128)(2,1)S(1)} %fusion.119), channel_id=1, source_target_pairs={{1,0},{2,1},{3,2},{4,3},{5,4},{6,5},{7,6},{8,7},{9,8},{10,9},{11,1... | collective-permute-start | bytes 3145736 | tf_op jit(solution)/shard_map/ppermute | solution.py:17
  57.2 84.0 %copy-start = (bf16[8,256,256]{2,1,0:T(8,128)(2,1)S(1)}, bf16[8,256,256]{2,1,0:T(8,128)(2,1)}, u32[]{:S(2)}) copy-start(bf16[8,256,256]{2,1,0:T(8,128)(2,1)} %param.8) | copy-start | bytes 3145732
  57.2 103.0 %copy-start.5 = (bf16[8,256,256]{2,1,0:T(8,128)(2,1)S(1)}, bf16[8,256,256]{2,1,0:T(8,128)(2,1)}, u32[]{:S(2)}) copy-start(bf16[8,256,256]{2,1,0:T(8,128)(2,1)} %param.13) | copy-start | bytes 3145732
  57.3 254.5 %all-reduce.6.cloned.1.call-start = ((), (), s32[]{:S(2)}) async-start(), calls=%async_computation.1 | async-start | bytes 4194304 | tf_op jit(solution)/shard_map/psum | solution.py:72
  141.2 19.1 %copy-start.1 = (f32[8,256,256]{2,1,0:T(8,128)S(1)}, f32[8,256,256]{2,1,0:T(8,128)}, u32[]{:S(2)}) copy-start(f32[8,256,256]{2,1,0:T(8,128)} %all-reduce.4.cloned.1.call-done) | copy-start | bytes 6291460
  144.3 1.2 collective-permute-start.6
  146.7 3.6 collective-permute-start.7
  150.9 3.6 collective-permute-start.8
  155.2 4.5 collective-permute-start.9
  160.3 17.7 %copy-start.6 = (bf16[8,256,256]{2,1,0:T(8,128)(2,1)S(1)}, bf16[8,256,256]{2,1,0:T(8,128)(2,1)}, u32[]{:S(2)}) copy-start(bf16[8,256,256]{2,1,0:T(8,128)(2,1)} %param.13) | copy-start | bytes 3145732
  161.9 1.3 collective-permute-start.10
  164.5 3.6 collective-permute-start.11
  168.7 3.6 collective-permute-start.12
  172.9 4.5 collective-permute-start.13
  180.0 1.2 collective-permute-start.14
  182.5 3.6 collective-permute-start.15
  186.7 3.6 collective-permute-start.16
  191.0 4.5 collective-permute-start.17
  196.3 3.6 collective-permute-start.18
  197.7 6.2 %collective-permute-start.19 = (bf16[8,256,256]{2,1,0:T(8,128)(2,1)S(1)}, bf16[8,256,256]{2,1,0:T(8,128)(2,1)S(1)}, u32[]{:S(2)}, u32[]{:S(2)}) collective-permute-start(bf16[8,256,256]{2,1,0:T(8,128)(2,1)S(1)} %fusion.120), channel_id=1, source_target_pairs={{1,0},{2,1},{3,2},{4,3},{5,4},{6,5},{7,6},{8,7},{9,8},{10,9},{11,1... | collective-permute-start | bytes 3145736 | tf_op jit(solution)/shard_map/ppermute | solution.py:17
  229.4 255.5 %all-reduce.8.cloned.1.call-start = ((), (), s32[]{:S(2)}) async-start(), calls=%async_computation.2 | async-start | bytes 4194304 | tf_op jit(solution)/shard_map/psum | solution.py:72
  311.8 19.4 %copy-start.2 = (f32[8,256,256]{2,1,0:T(8,128)S(1)}, f32[8,256,256]{2,1,0:T(8,128)}, u32[]{:S(2)}) copy-start(f32[8,256,256]{2,1,0:T(8,128)} %all-reduce.6.cloned.1.call-done) | copy-start | bytes 6291460
  311.8 19.4 %copy-start.7 = (bf16[8,256,256]{2,1,0:T(8,128)(2,1)S(1)}, bf16[8,256,256]{2,1,0:T(8,128)(2,1)}, u32[]{:S(2)}) copy-start(bf16[8,256,256]{2,1,0:T(8,128)(2,1)} %param.13) | copy-start | bytes 3145732
  314.8 1.5 collective-permute-start.20
  317.4 3.7 collective-permute-start.21
  321.7 3.7 collective-permute-start.22
  326.0 4.6 collective-permute-start.23
  335.1 1.2 collective-permute-start.24
  337.5 3.6 collective-permute-start.25
  342.4 3.6 collective-permute-start.26
  346.0 4.5 collective-permute-start.27
  354.5 1.4 collective-permute-start.28
  357.1 3.7 collective-permute-start.29
  361.4 3.7 collective-permute-start.30
  365.7 4.6 collective-permute-start.31
  372.6 3.6 collective-permute-start.32
  374.0 6.2 %collective-permute-start.33 = (bf16[8,256,256]{2,1,0:T(8,128)(2,1)S(1)}, bf16[8,256,256]{2,1,0:T(8,128)(2,1)S(1)}, u32[]{:S(2)}, u32[]{:S(2)}) collective-permute-start(bf16[8,256,256]{2,1,0:T(8,128)(2,1)S(1)} %get-tuple-element.13), channel_id=1, source_target_pairs={{1,0},{2,1},{3,2},{4,3},{5,4},{6,5},{7,6},{8,7},{9,8},{10,9},{11,1... | collective-permute-start | bytes 3145736 | tf_op jit(solution)/shard_map/ppermute | solution.py:17
  495.5 1.2 collective-permute-start.34
  496.7 3.6 collective-permute-start.35
  500.2 3.6 collective-permute-start.36
  503.8 4.5 collective-permute-start.37
  (14 other events, 39.5 us)
Sparse Core Ops, SparseCore 0:
  57.4 83.7 all-reduce.3
  229.6 82.1 all-reduce.5
  402.7 82.1 all-reduce.7
